TPU v7x, 32 devices: a whole 2x2x4 slice. The times are simulated.
32 devices in a mesh: seq: 2 (over y), row: 4 (over x, core), col: 4 (over z).
Axes of the slice: x: 2, y: 2, z: 4, core: 2. Of those that a mesh axis runs over, the one named last changes fastest.
Arguments:
- tokens: bfloat16 [4096, 5376], P(('seq', 'row'), 'col'), may hold values from -6 to 6
- w_query: bfloat16 [5376, 4096], P(('seq', 'row'), 'col'), may hold values from -0.078125 to 0.078125
- key_weight: bfloat16 [5376, 2048], P(('seq', 'row'), 'col'), may hold values from -0.078125 to 0.078125
- value_weight: bfloat16 [5376, 2048], P(('seq', 'row'), 'col'), may hold values from -0.078125 to 0.078125
- w_output: bfloat16 [4096, 5376], P(('seq', 'row'), 'col'), may hold values from -0.09375 to 0.09375
- query_gain: float32 [128], replicated, may hold values from 0.5 to 8
- key_gain: float32 [128], replicated, may hold values from 0.5 to 8
Outputs:
- attended: bfloat16 [4096, 5376], P(('seq', 'row'), 'col')
All inputs are finite; a program needn't handle non-finite values.
Results may differ from a plain program's by a relative error of at most 0.0085.
The roundings to bfloat16 on the way count: a program that leaves them out, or rounds other values in their place, can miss the bound.
Values may be sent and summed in bfloat16 or wider, within the bound.
A program may use at most 128 MiB of HBM per device.

v0:
```python
import jax
import jax.numpy as jnp
from jax import lax
from jax.sharding import PartitionSpec as P

HEAD_SIZE = 128
WINDOW_KEYS = 1024
query_scale = 168.0 ** (-0.5)


def shifted(block, axis, distance):
    devices = range(lax.axis_size(axis))
    route = [(i - distance, i) for i in devices if i - distance in devices]
    return lax.ppermute(block, axis, route)


def head_norm(block, gain):
    mean_square = jnp.mean(block * block, axis=-1, keepdims=True)
    return block * lax.rsqrt(mean_square + 1e-06) * gain


def rotate(block, positions):
    half = block.shape[-1] // 2
    freqs = 10000.0 ** (-(jnp.arange(half, dtype=jnp.float32) * 2.0 / block.shape[-1]))
    angles = positions.astype(jnp.float32)[:, None] * freqs[None, :]
    cosine = jnp.cos(angles)[:, None, :]
    sine = jnp.sin(angles)[:, None, :]
    first = block[..., :half]
    second = block[..., half:]
    return jnp.concatenate(
        [first * cosine - second * sine, second * cosine + first * sine], axis=-1
    )


def attend(queries, key_states, value_states, qpos, kpos):
    rows = queries.shape[0]
    kv_heads = key_states.shape[1]
    grouped = queries.reshape(rows, kv_heads, 2, HEAD_SIZE)
    scores = (
        jnp.einsum("bhgd,khd->hgbk", grouped, key_states, preferred_element_type=jnp.float32)
        * query_scale
    )
    gap = qpos[:, None] - kpos[None, :]
    valid = (kpos[None, :] >= 0) & (gap >= 0) & (gap < WINDOW_KEYS)
    scores = jnp.where(valid[None, None], scores, -1e30)
    top = jnp.max(scores, axis=-1, keepdims=True)
    weights = jnp.exp(scores - top)
    weights = (weights / jnp.sum(weights, axis=-1, keepdims=True)).astype(jnp.bfloat16)
    mixed = jnp.einsum("hgbk,khd->bhgd", weights, value_states, preferred_element_type=jnp.float32)
    return mixed.astype(jnp.bfloat16).reshape(rows, kv_heads * 2 * HEAD_SIZE)


def shards(tokens, w_query, key_weight, value_weight, w_output, query_gain, key_gain):
    rows = tokens.shape[0]
    whole = lax.all_gather(tokens, "col", axis=1, tiled=True)
    columns = whole
    proj_q = jnp.dot(
        columns,
        lax.all_gather(w_query, ("seq", "row"), axis=0, tiled=True),
        preferred_element_type=jnp.float32,
    )
    projected_key = jnp.dot(
        columns,
        lax.all_gather(key_weight, ("seq", "row"), axis=0, tiled=True),
        preferred_element_type=jnp.float32,
    )
    proj_v = jnp.dot(
        columns,
        lax.all_gather(value_weight, ("seq", "row"), axis=0, tiled=True),
        preferred_element_type=jnp.float32,
    )
    base = lax.axis_index(("seq", "row")) * rows
    positions = base + jnp.arange(rows, dtype=jnp.int32)
    q_heads = proj_q.shape[1] // HEAD_SIZE
    kv_heads = projected_key.shape[1] // HEAD_SIZE
    queries = rotate(
        head_norm(proj_q.reshape(rows, q_heads, HEAD_SIZE), query_gain), positions
    ).astype(jnp.bfloat16)
    key_states = rotate(
        head_norm(projected_key.reshape(rows, kv_heads, HEAD_SIZE), key_gain), positions
    ).astype(jnp.bfloat16)
    key_flat = key_states.reshape(rows, kv_heads * HEAD_SIZE)
    value_flat = proj_v.astype(jnp.bfloat16)
    prior_one = shifted((key_flat, value_flat), ("seq", "row"), 1)
    prior_two = shifted((key_flat, value_flat), ("seq", "row"), 2)
    key_rows = jnp.concatenate([prior_two[0], prior_one[0], key_flat], axis=0).reshape(
        3 * rows, kv_heads, HEAD_SIZE
    )
    value_rows = jnp.concatenate([prior_two[1], prior_one[1], value_flat], axis=0).reshape(
        3 * rows, kv_heads, HEAD_SIZE
    )
    kpos = base - 2 * rows + jnp.arange(3 * rows, dtype=jnp.int32)
    mixed = attend(queries, key_rows, value_rows, positions, kpos)
    all_heads = lax.all_gather(mixed, "col", axis=1, tiled=True)
    columns = all_heads
    attended = jnp.dot(
        columns,
        lax.all_gather(w_output, ("seq", "row"), axis=0, tiled=True),
        preferred_element_type=jnp.float32,
    )
    return attended.astype(jnp.bfloat16)


def solution(mesh):
    return jax.shard_map(
        shards,
        mesh=mesh,
        in_specs=(
            P(("seq", "row"), "col"),
            P(("seq", "row"), "col"),
            P(("seq", "row"), "col"),
            P(("seq", "row"), "col"),
            P(("seq", "row"), "col"),
            P(),
            P(),
        ),
        out_specs=P(("seq", "row"), "col"),
        check_vma=False,
    )
```

profile of v0, /device:TPU:0, one launch (start us, length us, event | category | flops | bytes accessed | tf_op | source)
XLA Modules:
  0.0 458.2 jit_solution(17075732382961147357)
XLA Ops:
  6.5 0.7 all-gather.7.cloned.1.call-update
  7.3 0.7 all-gather.11.cloned.1.call-update
  8.1 0.7 all-gather.9.cloned.1.call-update
  9.4 0.5 all-gather.17.cloned.1.call-update
  10.0 1.0 multiply_cosine_fusion
  11.0 103.0 %all-gather.7.cloned.1.call-done = bf16[512,5376]{0,1:T(8,128)(2,1)} async-done(((bf16[512,1344]{0,1:T(8,128)(2,1)}), bf16[512,5376]{0,1:T(8,128)(2,1)}) %all-gather.7.cloned.1.call-update) | async-done | bytes 5505040 | tf_op jit(solution)/shard_map/all_gather | solution.py:55
  114.0 42.5 %all-gather.11.cloned.1.call-done = bf16[5376,512]{1,0:T(8,128)(2,1)} async-done(((bf16[672,512]{1,0:T(8,128)(2,1)}), bf16[5376,512]{1,0:T(8,128)(2,1)}) %all-gather.11.cloned.1.call-update) | async-done | bytes 5505040 | tf_op jit(solution)/shard_map/all_gather | solution.py:64
  156.5 6.7 %multiply_reduce_fusion.1 = (f32[512,4]{0,1:T(4,128)S(1)}, f32[512,512]{0,1:T(8,128)S(1)}) fusion(bf16[512,5376]{0,1:T(8,128)(2,1)} %all-gather.7.cloned.1.call-done, bf16[5376,512]{1,0:T(8,128)(2,1)} %all-gather.11.cloned.1.call-done), kind=kOutput, calls=%fused_computation.29 | convolution fusion | flops 2819094528 | bytes 12066816 | tf_op jit(solution)/shard_map/dot_general | solution.py:62
  164.9 3.4 collective-permute-start.2
  168.3 1.9 collective-permute-start.3
  170.3 39.0 %all-gather.9.cloned.1.call-done = bf16[5376,512]{1,0:T(8,128)(2,1)} async-done(((bf16[672,512]{1,0:T(8,128)(2,1)}), bf16[5376,512]{1,0:T(8,128)(2,1)}) %all-gather.9.cloned.1.call-update) | async-done | bytes 5505040 | tf_op jit(solution)/shard_map/all_gather | solution.py:69
  209.3 7.2 %convolution_convert_fusion.1 = bf16[512,512]{1,0:T(8,128)(2,1)S(1)} fusion(bf16[512,5376]{0,1:T(8,128)(2,1)} %all-gather.7.cloned.1.call-done, bf16[5376,512]{1,0:T(8,128)(2,1)} %all-gather.9.cloned.1.call-done), kind=kOutput, calls=%fused_computation.23 | convolution fusion | flops 2818834432 | bytes 11534336 | tf_op jit(solution)/shard_map/dot_general | solution.py:67
  216.5 3.1 collective-permute-start
  219.6 2.7 collective-permute-start.1
  222.2 2.0 fusion.9
  224.2 1.0 copy.32
  225.2 1.0 copy.33
  226.2 15.8 %collective-permute-done = bf16[512,512]{1,0:T(8,128)(2,1)} collective-permute-done((bf16[512,512]{1,0:T(8,128)(2,1)S(1)}, bf16[512,512]{1,0:T(8,128)(2,1)}, u32[]{:S(2)}, u32[]{:S(2)}) %collective-permute-start) | collective-permute-done | bytes 524320 | tf_op jit(solution)/shard_map/ppermute | solution.py:14
  242.0 1.3 pad_maximum_fusion
  243.3 1.6 copy.43
  244.9 44.2 %all-gather.13.cloned.1.call-done = bf16[5376,1024]{1,0:T(8,128)(2,1)} async-done(((bf16[672,1024]{1,0:T(8,128)(2,1)}), bf16[5376,1024]{1,0:T(8,128)(2,1)}) %all-gather.13.cloned.1.call-update) | async-done | bytes 11010064 | tf_op jit(solution)/shard_map/all_gather | solution.py:59
  289.1 10.3 %convolution_bitcast_fusion = f32[64,8,8,128]{3,1,2,0:T(8,128)S(1)} fusion(bf16[512,5376]{0,1:T(8,128)(2,1)} %all-gather.7.cloned.1.call-done, bf16[5376,1024]{1,0:T(8,128)(2,1)} %all-gather.13.cloned.1.call-done), kind=kOutput, calls=%fused_computation.19 | convolution fusion | flops 5637144576 | bytes 18612224 | tf_op jit(solution)/shard_map/dot_general | solution.py:57
  299.9 0.6 multiply_reduce_fusion
  300.8 0.9 multiply_multiply_fusion
  301.6 0.9 subtract_convert_fusion
  302.8 0.7 copy-done
  303.7 11.8 %fusion.11 = f32[4,1536,512,2]{2,1,3,0:T(8,128)} fusion(bf16[512,4,128]{2,0,1:T(8,128)(2,1)S(1)} %maximum_convert_fusion, bf16[512,4,128]{2,0,1:T(8,128)(2,1)S(1)} %copy-done.1, bf16[512,4,128]{2,0,1:T(8,128)(2,1)S(1)} %copy-done, bf16[512,4,2,64]{3,0,2,1:T(8,128)(2,1)S(1)} %bitcast.51, bf16[512,4,2,64]{3,0,2,1:T(8,128)(2,1)S(1)} %bitcast.53), kind=kOutput, calls=%fused_computation.30 | convolution fusion | flops 1617428480 | bytes 27787264 | tf_op jit(solution)/shard_map/bhgd,khd->hgbk/dot_general | solution.py:40
  315.6 10.5 %fusion.23 = f32[4,2,512]{2,1,0:T(2,128)S(1)} fusion(pred[512,1536]{0,1:T(8,128)(4,1)} %fusion.9, bf16[512,4,128]{2,0,1:T(8,128)(2,1)S(1)} %maximum_convert_fusion, bf16[512,4,128]{2,0,1:T(8,128)(2,1)} %copy.33, bf16[512,4,128]{2,0,1:T(8,128)(2,1)S(1)} %copy-done, bf16[512,4,2,64]{3,0,2,1:T(8,128)(2,1)S(1)} %bitcast.52, bf16[512,4,2,64]{3,0,2,1:T(8,128)(2,1)S(1)} %bitcast.54), kind=kOutput, calls=%fused_computation.47 | convolution fusion | flops 1642595840 | bytes 3424256 | tf_op jit(solution)/shard_map/sub | solution.py:47
  326.1 15.4 %fusion.10 = bf16[4,128,2,512]{3,1,2,0:T(8,128)(2,1)} fusion(bf16[1536,4,128,1]{0,2,3,1:T(8,128)(2,1)} %bitcast.55, f32[4,2,512]{2,1,0:T(2,128)S(1)} %fusion.23, f32[4,1536,512,2]{2,1,3,0:T(8,128)} %fusion.11, pred[512,1536]{0,1:T(8,128)(4,1)} %fusion.9), kind=kOutput, calls=%fused_computation.22 | convolution fusion | flops 1642599936 | bytes 28590080 | tf_op jit(solution)/shard_map/hgbk,khd->bhgd/dot_general | solution.py:49
  341.5 17.0 %all-gather.17.cloned.1.call-done = bf16[4096,1344]{0,1:T(8,128)(2,1)} async-done(((bf16[512,1344]{0,1:T(8,128)(2,1)}), bf16[4096,1344]{0,1:T(8,128)(2,1)}) %all-gather.17.cloned.1.call-update) | async-done | bytes 11010064 | tf_op jit(solution)/shard_map/all_gather | solution.py:98
  358.5 82.2 %all-gather.15.cloned.1.call-done = bf16[512,4096]{0,1:T(8,128)(2,1)} async-done(((bf16[512,1024]{0,1:T(8,128)(2,1)}), bf16[512,4096]{0,1:T(8,128)(2,1)}) %all-gather.15.cloned.1.call-update) | async-done | bytes 4194320 | tf_op jit(solution)/shard_map/all_gather | solution.py:94
  440.7 10.7 %convolution_convert_fusion = bf16[512,1344]{0,1:T(8,128)(2,1)} fusion(bf16[4096,1344]{0,1:T(8,128)(2,1)} %all-gather.17.cloned.1.call-done, bf16[512,4096]{0,1:T(8,128)(2,1)} %all-gather.15.cloned.1.call-done), kind=kOutput, calls=%fused_computation.14 | convolution fusion | flops 5637832704 | bytes 16580608 | tf_op jit(solution)/shard_map/dot_general | solution.py:96
  (35 shorter events, 3.6 us)
Async XLA Ops:
  6.5 107.5 %all-gather.7.cloned.1.call-start = ((), (), s32[]{:S(2)}) async-start(), calls=%async_computation | async-start | bytes 6881280 | tf_op jit(solution)/shard_map/all_gather | solution.py:55
  7.3 149.3 %all-gather.11.cloned.1.call-start = ((), (), s32[]{:S(2)}) async-start(), calls=%async_computation.2 | async-start | bytes 6193152 | tf_op jit(solution)/shard_map/all_gather | solution.py:64
  8.0 201.3 %all-gather.9.cloned.1.call-start = ((), (), s32[]{:S(2)}) async-start(), calls=%async_computation.1 | async-start | bytes 6193152 | tf_op jit(solution)/shard_map/all_gather | solution.py:69
  8.7 280.4 %all-gather.13.cloned.1.call-start = ((), (), s32[]{:S(2)}) async-start(), calls=%async_computation.3 | async-start | bytes 12386304 | tf_op jit(solution)/shard_map/all_gather | solution.py:59
  9.3 349.2 %all-gather.17.cloned.1.call-start = ((), (), s32[]{:S(2)}) async-start(), calls=%async_computation.5 | async-start | bytes 12386304 | tf_op jit(solution)/shard_map/all_gather | solution.py:98
  9.9 430.8 %all-gather.15.cloned.1.call-start = ((), (), s32[]{:S(2)}) async-start(), calls=%async_computation.4 | async-start | bytes 5242880 | tf_op jit(solution)/shard_map/all_gather | solution.py:94
  11.0 152.6 %copy-start.2 = (f32[128]{0:T(128)S(1)}, f32[128]{0:T(128)}, u32[]{:S(2)}) copy-start(f32[128]{0:T(128)} %param.13) | copy-start | bytes 1540
  164.9 59.3 %collective-permute-start.2 = (bf16[512,512]{0,1:T(8,128)(2,1)S(1)}, bf16[512,512]{0,1:T(8,128)(2,1)S(1)}, u32[]{:S(2)}, u32[]{:S(2)}) collective-permute-start(bf16[512,512]{0,1:T(8,128)(2,1)S(1)} %bitcast.58), channel_id=1, source_target_pairs={{0,8},{4,12},{8,16},{12,20},{16,24},{20,28},{1,9},{5,13},{9,17},{1... | collective-permute-start | bytes 1572872 | tf_op jit(solution)/shard_map/ppermute | solution.py:14
  168.3 56.9 %collective-permute-start.3 = (bf16[512,512]{0,1:T(8,128)(2,1)S(1)}, bf16[512,512]{0,1:T(8,128)(2,1)S(1)}, u32[]{:S(2)}, u32[]{:S(2)}) collective-permute-start(bf16[512,512]{0,1:T(8,128)(2,1)S(1)} %bitcast.59), channel_id=1, source_target_pairs={{0,4},{4,8},{8,12},{12,16},{16,20},{20,24},{24,28},{1,5},{5,9},{9,... | collective-permute-start | bytes 1572872 | tf_op jit(solution)/shard_map/ppermute | solution.py:14
  216.5 25.5 %collective-permute-start = (bf16[512,512]{1,0:T(8,128)(2,1)S(1)}, bf16[512,512]{1,0:T(8,128)(2,1)}, u32[]{:S(2)}, u32[]{:S(2)}) collective-permute-start(bf16[512,512]{1,0:T(8,128)(2,1)S(1)} %convolution_convert_fusion.1), channel_id=1, source_target_pairs={{0,8},{4,12},{8,16},{12,20},{16,24},{20,28},{1,9},{5,13},{9,17},{1... | collective-permute-start | bytes 1572872 | tf_op jit(solution)/shard_map/ppermute | solution.py:14
  219.6 22.5 %collective-permute-start.1 = (bf16[512,512]{1,0:T(8,128)(2,1)S(1)}, bf16[512,512]{1,0:T(8,128)(2,1)}, u32[]{:S(2)}, u32[]{:S(2)}) collective-permute-start(bf16[512,512]{1,0:T(8,128)(2,1)S(1)} %convolution_convert_fusion.1), channel_id=1, source_target_pairs={{0,4},{4,8},{8,12},{12,16},{16,20},{20,24},{24,28},{1,5},{5,9},{9,... | collective-permute-start | bytes 1572872 | tf_op jit(solution)/shard_map/ppermute | solution.py:14
  299.4 1.4 copy-start.3
  302.5 1.1 copy-start
  302.5 1.2 copy-start.1
Sparse Core Ops, SparseCore 0:
  8.9 105.0 all-gather.6
  115.9 40.5 all-gather.10
  158.4 50.8 all-gather.8
  211.0 78.0 all-gather.12
  290.8 67.6 all-gather.16
  359.9 80.7 all-gather.14
where the time goes:
time: 458 us
  waiting for transfers between devices  347 us (76%)
  matrix products  72.6 us (16%)
  between operations  13.7 us (3%)
  starting transfers between devices  11.2 us (2%)
  other arithmetic  7.75 us (2%)
  local copies, waits for them, and re-layouts  6.03 us (1%)
    all_gather x1, waiting for transfers between devices, shards(): whole = lax.all_gather(tokens, 'col', axis=1, tiled=True)  103 us
    all_gather x1, waiting for transfers between devices, shards(): all_heads = lax.all_gather(mixed, 'col', axis=1, tiled=True)  82.2 us
    all_gather x1, waiting for transfers between devices, shards(): lax.all_gather(w_query, ('seq', 'row'), axis=0, tiled=True)  44.2 us
    all_gather x1, waiting for transfers between devices, shards(): lax.all_gather(key_weight, ('seq', 'row'), axis=0, tiled=True)  42.5 us
    all_gather x1, waiting for transfers between devices, shards(): lax.all_gather(value_weight, ('seq', 'row'), axis=0, tiled=True)  39 us
    all_gather x1, waiting for transfers between devices, shards(): lax.all_gather(w_output, ('seq', 'row'), axis=0, tiled=True)  17 us
    ppermute x4, waiting for transfers between devices, shifted(): return lax.ppermute(block, axis, route)  15.8 us
    dot_general x1, matrix products, attend(): jnp.einsum('hgbk,khd->bhgd', weights, value_states, preferred_element_typ...  15.4 us
  transfers between devices with their start and end apart: 10, of which 7 were waited for; matrix products, arithmetic and copies ran while one was open for 16% of the time, Pallas kernels for 0%

commit v1 on v0

--- a/solution.py
+++ b/solution.py
@@ -91,7 +91,12 @@
     )
     kpos = base - 2 * rows + jnp.arange(3 * rows, dtype=jnp.int32)
     mixed = attend(queries, key_rows, value_rows, positions, kpos)
-    all_heads = lax.all_gather(mixed, "col", axis=1, tiled=True)
+    ring = [mixed]
+    for hop in range(3):
+        ring.append(lax.ppermute(ring[-1], "col", [(dev, (dev + 1) % 4) for dev in range(4)]))
+    all_heads = jnp.roll(
+        jnp.concatenate(ring[::-1], axis=1), (lax.axis_index("col") + 1) * ring[0].shape[1], axis=1
+    )
     columns = all_heads
     attended = jnp.dot(
         columns,

time: 458 us -> 448 us (0.978)
  waiting for transfers between devices: 347 us -> 325 us
  local copies, waits for them, and re-layouts: 6.03 us -> 16.2 us
    all_gather x1 -> x0, waiting for transfers between devices: 82.2 us -> none  [shards(): all_heads = lax.all_gather(mixed, 'col', axis=1, tiled=True)]
    ppermute x0 -> x3, waiting for transfers between devices: none -> 77.4 us  [shards(): lax.ppermute(ring[-1], 'col', [(dev, (dev + 1) % 4) for dev in range(4)])]
    all_gather x1, waiting for transfers between devices: 17 us -> 0.01 us  [shards(): lax.all_gather(w_output, ('seq', 'row'), axis=0, tiled=True)]
    unnamed x9 -> x18, local copies, waits for them, and re-layouts: 1.4 us -> 10.4 us
  transfers between devices with their start and end apart: 10 -> 12, of which waited for: 7 -> 8; matrix products, arithmetic and copies ran while one was open for 16% -> 19% of each run, Pallas kernels for 0% -> 0%
where the time goes in v1:
time: 448 us; the launch traced here: 447 us
  waiting for transfers between devices  325 us (73%)
  matrix products  72.1 us (16%)
  local copies, waits for them, and re-layouts  16.2 us (4%)
  between operations  13.4 us (3%)
  starting transfers between devices  12.8 us (3%)
  other arithmetic  7.73 us (2%)
    all_gather x1, waiting for transfers between devices, shards(): whole = lax.all_gather(tokens, 'col', axis=1, tiled=True)  103 us
    ppermute x3, waiting for transfers between devices, shards(): lax.ppermute(ring[-1], 'col', [(dev, (dev + 1) % 4) for dev in range(4)])  77.4 us
    all_gather x1, waiting for transfers between devices, shards(): lax.all_gather(w_query, ('seq', 'row'), axis=0, tiled=True)  44.2 us
    all_gather x1, waiting for transfers between devices, shards(): lax.all_gather(key_weight, ('seq', 'row'), axis=0, tiled=True)  42.5 us
    all_gather x1, waiting for transfers between devices, shards(): lax.all_gather(value_weight, ('seq', 'row'), axis=0, tiled=True)  39 us
    ppermute x4, waiting for transfers between devices, shifted(): return lax.ppermute(block, axis, route)  15.8 us
    dot_general x1, matrix products, attend(): jnp.einsum('hgbk,khd->bhgd', weights, value_states, preferred_element_typ...  14.7 us
    dot_general x1, matrix products, attend(): jnp.einsum('bhgd,khd->hgbk', grouped, key_states, preferred_element_type=...  11.8 us
  transfers between devices with their start and end apart: 12, of which 8 were waited for; matrix products, arithmetic and copies ran while one was open for 19% of the time, Pallas kernels for 0%

profile of v1, /device:TPU:0, one launch (start us, length us, event | category | flops | bytes accessed | tf_op | source)
XLA Modules:
  0.0 447.3 jit_solution(10434675050669129227)
XLA Ops:
  11.0 103.1 %all-gather.6.cloned.1.call-done = bf16[512,5376]{0,1:T(8,128)(2,1)} async-done(((bf16[512,1344]{0,1:T(8,128)(2,1)}), bf16[512,5376]{0,1:T(8,128)(2,1)}) %all-gather.6.cloned.1.call-update) | async-done | bytes 5505040 | tf_op jit(solution)/shard_map/all_gather | solution.py:55
  114.0 42.5 %all-gather.10.cloned.1.call-done = bf16[5376,512]{1,0:T(8,128)(2,1)} async-done(((bf16[672,512]{1,0:T(8,128)(2,1)}), bf16[5376,512]{1,0:T(8,128)(2,1)}) %all-gather.10.cloned.1.call-update) | async-done | bytes 5505040 | tf_op jit(solution)/shard_map/all_gather | solution.py:64
  156.5 6.7 %multiply_reduce_fusion.1 = (f32[512,4]{0,1:T(4,128)S(1)}, f32[512,512]{0,1:T(8,128)S(1)}) fusion(bf16[512,5376]{0,1:T(8,128)(2,1)} %all-gather.6.cloned.1.call-done, bf16[5376,512]{1,0:T(8,128)(2,1)} %all-gather.10.cloned.1.call-done), kind=kOutput, calls=%fused_computation.31 | convolution fusion | flops 2819094528 | bytes 12066816 | tf_op jit(solution)/shard_map/dot_general | solution.py:62
  164.9 3.4 collective-permute-start.2
  168.3 1.9 collective-permute-start.3
  170.3 39.0 %all-gather.8.cloned.1.call-done = bf16[5376,512]{1,0:T(8,128)(2,1)} async-done(((bf16[672,512]{1,0:T(8,128)(2,1)}), bf16[5376,512]{1,0:T(8,128)(2,1)}) %all-gather.8.cloned.1.call-update) | async-done | bytes 5505040 | tf_op jit(solution)/shard_map/all_gather | solution.py:69
  209.3 7.2 %convolution_convert_fusion = bf16[512,512]{1,0:T(8,128)(2,1)S(1)} fusion(bf16[512,5376]{0,1:T(8,128)(2,1)} %all-gather.6.cloned.1.call-done, bf16[5376,512]{1,0:T(8,128)(2,1)} %all-gather.8.cloned.1.call-done), kind=kOutput, calls=%fused_computation.25 | convolution fusion | flops 2818834432 | bytes 11534336 | tf_op jit(solution)/shard_map/dot_general | solution.py:67
  216.5 3.1 collective-permute-start
  219.6 2.7 collective-permute-start.1
  222.2 2.0 fusion.11
  224.2 1.0 copy.32
  226.3 15.8 %collective-permute-done = bf16[512,512]{1,0:T(8,128)(2,1)} collective-permute-done((bf16[512,512]{1,0:T(8,128)(2,1)S(1)}, bf16[512,512]{1,0:T(8,128)(2,1)}, u32[]{:S(2)}, u32[]{:S(2)}) %collective-permute-start) | collective-permute-done | bytes 524320 | tf_op jit(solution)/shard_map/ppermute | solution.py:14
  242.0 1.3 pad_maximum_fusion
  243.3 1.6 copy.43
  244.9 44.2 %all-gather.12.cloned.1.call-done = bf16[5376,1024]{1,0:T(8,128)(2,1)} async-done(((bf16[672,1024]{1,0:T(8,128)(2,1)}), bf16[5376,1024]{1,0:T(8,128)(2,1)}) %all-gather.12.cloned.1.call-update) | async-done | bytes 11010064 | tf_op jit(solution)/shard_map/all_gather | solution.py:59
  289.1 10.3 %convolution_bitcast_fusion = f32[64,8,8,128]{3,1,2,0:T(8,128)S(1)} fusion(bf16[512,5376]{0,1:T(8,128)(2,1)} %all-gather.6.cloned.1.call-done, bf16[5376,1024]{1,0:T(8,128)(2,1)} %all-gather.12.cloned.1.call-done), kind=kOutput, calls=%fused_computation.21 | convolution fusion | flops 5637144576 | bytes 18612224 | tf_op jit(solution)/shard_map/dot_general | solution.py:57
  302.9 11.8 %fusion.16 = f32[4,1536,512,2]{2,1,3,0:T(8,128)} fusion(bf16[512,4,128]{2,0,1:T(8,128)(2,1)S(1)} %maximum_convert_fusion, bf16[512,4,128]{2,0,1:T(8,128)(2,1)S(1)} %copy-done.2, bf16[512,4,128]{2,0,1:T(8,128)(2,1)S(1)} %copy-done, bf16[512,4,2,64]{3,0,2,1:T(8,128)(2,1)S(1)} %bitcast.50, bf16[512,4,2,64]{3,0,2,1:T(8,128)(2,1)S(1)} %bitcast.52), kind=kOutput, calls=%fused_computation.32 | convolution fusion | flops 1617428480 | bytes 27787264 | tf_op jit(solution)/shard_map/bhgd,khd->hgbk/dot_general | solution.py:40
  314.7 10.8 %fusion.29 = f32[4,2,512]{2,1,0:T(2,128)S(1)} fusion(pred[512,1536]{0,1:T(8,128)(4,1)} %fusion.11, bf16[512,4,128]{2,0,1:T(8,128)(2,1)S(1)} %maximum_convert_fusion, bf16[512,4,128]{2,0,1:T(8,128)(2,1)} %copy.33, bf16[512,4,128]{2,0,1:T(8,128)(2,1)S(1)} %copy-done.1, bf16[512,4,2,64]{3,0,2,1:T(8,128)(2,1)S(1)} %bitcast.51, ...), kind=kOutput, calls=%fused_computation.58 | convolution fusion | flops 1642595840 | bytes 3424256 | tf_op jit(solution)/shard_map/sub | solution.py:47
  325.5 14.7 %fusion.15 = bf16[4,128,2,512]{3,1,2,0:T(8,128)(2,1)S(1)} fusion(bf16[1536,4,128,1]{0,2,3,1:T(8,128)(2,1)} %bitcast.57, f32[4,2,512]{2,1,0:T(2,128)S(1)} %fusion.29, f32[4,1536,512,2]{2,1,3,0:T(8,128)} %fusion.16, pred[512,1536]{0,1:T(8,128)(4,1)} %fusion.11), kind=kOutput, calls=%fused_computation.24 | convolution fusion | flops 1642599936 | bytes 28590080 | tf_op jit(solution)/shard_map/hgbk,khd->bhgd/dot_general | solution.py:49
  340.1 1.6 collective-permute-start.4
  341.7 25.6 %collective-permute-done.4 = bf16[512,1024]{0,1:T(8,128)(2,1)S(1)} collective-permute-done((bf16[512,1024]{0,1:T(8,128)(2,1)S(1)}, bf16[512,1024]{0,1:T(8,128)(2,1)S(1)}, u32[]{:S(2)}, u32[]{:S(2)}) %collective-permute-start.4) | collective-permute-done | bytes 1048608 | tf_op jit(solution)/shard_map/ppermute | solution.py:96
  367.3 26.3 %collective-permute-done.5 = bf16[512,1024]{0,1:T(8,128)(2,1)S(1)} collective-permute-done((bf16[512,1024]{0,1:T(8,128)(2,1)S(1)}, bf16[512,1024]{0,1:T(8,128)(2,1)S(1)}, u32[]{:S(2)}, u32[]{:S(2)}) %collective-permute-start.5) | collective-permute-done | bytes 1048608 | tf_op jit(solution)/shard_map/ppermute | solution.py:96
  393.6 25.5 %collective-permute-done.6 = bf16[512,1024]{0,1:T(8,128)(2,1)} collective-permute-done((bf16[512,1024]{0,1:T(8,128)(2,1)S(1)}, bf16[512,1024]{0,1:T(8,128)(2,1)}, u32[]{:S(2)}, u32[]{:S(2)}) %collective-permute-start.6) | collective-permute-done | bytes 1048608 | tf_op jit(solution)/shard_map/ppermute | solution.py:96
  419.1 2.3 constant_dynamic-update-slice_fusion.7
  421.4 1.1 constant_dynamic-update-slice_fusion.6
  422.4 1.0 constant_dynamic-update-slice_fusion.5
  423.5 1.1 constant_dynamic-update-slice_fusion.4
  424.6 2.3 constant_dynamic-update-slice_fusion.3
  426.8 1.1 constant_dynamic-update-slice_fusion.2
  427.9 1.1 constant_dynamic-update-slice_fusion.1
  429.0 1.1 constant_dynamic-update-slice_fusion
  430.1 10.7 %fusion.12 = bf16[512,1344]{0,1:T(8,128)(2,1)} fusion(bf16[4096,1344]{0,1:T(8,128)(2,1)} %all-gather.14.cloned.1.call-done, bf16[512,8192]{0,1:T(8,128)(2,1)} %constant_dynamic-update-slice_fusion, s32[]{:T(128)S(6)} %select_n.19), kind=kOutput, calls=%fused_computation.16 | convolution fusion | flops 5637832704 | bytes 16580612 | tf_op jit(solution)/shard_map/dot_general | solution.py:101
  (48 shorter events, 10.4 us)
Async XLA Ops:
  6.5 107.5 %all-gather.6.cloned.1.call-start = ((), (), s32[]{:S(2)}) async-start(), calls=%async_computation | async-start | bytes 6881280 | tf_op jit(solution)/shard_map/all_gather | solution.py:55
  7.3 149.3 %all-gather.10.cloned.1.call-start = ((), (), s32[]{:S(2)}) async-start(), calls=%async_computation.2 | async-start | bytes 6193152 | tf_op jit(solution)/shard_map/all_gather | solution.py:64
  8.0 201.3 %all-gather.8.cloned.1.call-start = ((), (), s32[]{:S(2)}) async-start(), calls=%async_computation.1 | async-start | bytes 6193152 | tf_op jit(solution)/shard_map/all_gather | solution.py:69
  8.7 280.4 %all-gather.12.cloned.1.call-start = ((), (), s32[]{:S(2)}) async-start(), calls=%async_computation.3 | async-start | bytes 12386304 | tf_op jit(solution)/shard_map/all_gather | solution.py:59
  9.3 420.8 %all-gather.14.cloned.1.call-start = ((), (), s32[]{:S(2)}) async-start(), calls=%async_computation.4 | async-start | bytes 12386304 | tf_op jit(solution)/shard_map/all_gather | solution.py:103
  11.0 152.6 %copy-start.3 = (f32[128]{0:T(128)S(1)}, f32[128]{0:T(128)}, u32[]{:S(2)}) copy-start(f32[128]{0:T(128)} %param.13) | copy-start | bytes 1540
  164.9 59.3 %collective-permute-start.2 = (bf16[512,512]{0,1:T(8,128)(2,1)S(1)}, bf16[512,512]{0,1:T(8,128)(2,1)S(1)}, u32[]{:S(2)}, u32[]{:S(2)}) collective-permute-start(bf16[512,512]{0,1:T(8,128)(2,1)S(1)} %bitcast.59), channel_id=1, source_target_pairs={{0,8},{4,12},{8,16},{12,20},{16,24},{20,28},{1,9},{5,13},{9,17},{1... | collective-permute-start | bytes 1572872 | tf_op jit(solution)/shard_map/ppermute | solution.py:14
  168.3 56.9 %collective-permute-start.3 = (bf16[512,512]{0,1:T(8,128)(2,1)S(1)}, bf16[512,512]{0,1:T(8,128)(2,1)S(1)}, u32[]{:S(2)}, u32[]{:S(2)}) collective-permute-start(bf16[512,512]{0,1:T(8,128)(2,1)S(1)} %bitcast.60), channel_id=1, source_target_pairs={{0,4},{4,8},{8,12},{12,16},{16,20},{20,24},{24,28},{1,5},{5,9},{9,... | collective-permute-start | bytes 1572872 | tf_op jit(solution)/shard_map/ppermute | solution.py:14
  216.5 25.5 %collective-permute-start = (bf16[512,512]{1,0:T(8,128)(2,1)S(1)}, bf16[512,512]{1,0:T(8,128)(2,1)}, u32[]{:S(2)}, u32[]{:S(2)}) collective-permute-start(bf16[512,512]{1,0:T(8,128)(2,1)S(1)} %convolution_convert_fusion), channel_id=1, source_target_pairs={{0,8},{4,12},{8,16},{12,20},{16,24},{20,28},{1,9},{5,13},{9,17},{1... | collective-permute-start | bytes 1572872 | tf_op jit(solution)/shard_map/ppermute | solution.py:14
  219.6 22.5 %collective-permute-start.1 = (bf16[512,512]{1,0:T(8,128)(2,1)S(1)}, bf16[512,512]{1,0:T(8,128)(2,1)}, u32[]{:S(2)}, u32[]{:S(2)}) collective-permute-start(bf16[512,512]{1,0:T(8,128)(2,1)S(1)} %convolution_convert_fusion), channel_id=1, source_target_pairs={{0,4},{4,8},{8,12},{12,16},{16,20},{20,24},{24,28},{1,5},{5,9},{9,... | collective-permute-start | bytes 1572872 | tf_op jit(solution)/shard_map/ppermute | solution.py:14
  299.4 1.4 copy-start.4
  301.6 1.2 copy-start
  301.6 1.2 copy-start.2
  302.9 11.8 %copy-start.1 = (bf16[512,4,128]{2,0,1:T(8,128)(2,1)S(1)}, bf16[512,4,128]{2,0,1:T(8,128)(2,1)}, u32[]{:S(2)}) copy-start(bf16[512,4,128]{2,0,1:T(8,128)(2,1)} %copy.32) | copy-start | bytes 1572868
  340.1 27.2 %collective-permute-start.4 = (bf16[512,1024]{0,1:T(8,128)(2,1)S(1)}, bf16[512,1024]{0,1:T(8,128)(2,1)S(1)}, u32[]{:S(2)}, u32[]{:S(2)}) collective-permute-start(bf16[512,1024]{0,1:T(8,128)(2,1)S(1)} %bitcast.54), channel_id=1, source_target_pairs={{0,1},{1,2},{2,3},{3,0},{4,5},{5,6},{6,7},{7,4},{8,9},{9,10},{10,1... | collective-permute-start | bytes 3145736 | tf_op jit(solution)/shard_map/ppermute | solution.py:96
  367.3 26.3 %collective-permute-start.5 = (bf16[512,1024]{0,1:T(8,128)(2,1)S(1)}, bf16[512,1024]{0,1:T(8,128)(2,1)S(1)}, u32[]{:S(2)}, u32[]{:S(2)}) collective-permute-start(bf16[512,1024]{0,1:T(8,128)(2,1)S(1)} %collective-permute-done.4), channel_id=1, source_target_pairs={{0,1},{1,2},{2,3},{3,0},{4,5},{5,6},{6,7},{7,4},{8,9},{9,10},{10,1... | collective-permute-start | bytes 3145736 | tf_op jit(solution)/shard_map/ppermute | solution.py:96
  393.6 25.5 %collective-permute-start.6 = (bf16[512,1024]{0,1:T(8,128)(2,1)S(1)}, bf16[512,1024]{0,1:T(8,128)(2,1)}, u32[]{:S(2)}, u32[]{:S(2)}) collective-permute-start(bf16[512,1024]{0,1:T(8,128)(2,1)S(1)} %collective-permute-done.5), channel_id=1, source_target_pairs={{0,1},{1,2},{2,3},{3,0},{4,5},{5,6},{6,7},{7,4},{8,9},{9,10},{10,1... | collective-permute-start | bytes 3145736 | tf_op jit(solution)/shard_map/ppermute | solution.py:96
Sparse Core Ops, SparseCore 0:
  8.9 105.0 all-gather.5
  115.9 40.5 all-gather.9
  158.4 50.8 all-gather.7
  211.0 78.0 all-gather.11
  290.8 67.6 all-gather.13
